TPU v7x, 32 devices: a whole 2x2x4 slice. The times are simulated.
32 devices in a mesh: dp: 4 (over y, core), expert: 8 (over z, x).
Axes of the slice: x: 2, y: 2, z: 4, core: 2. Of those that a mesh axis runs over, the one named last changes fastest.
Arguments:
- tokens: bfloat16 [16384, 512], P(('dp', 'expert')), may hold values from -6 to 6
- remain: float32 [16384], P(('dp', 'expert')), may hold values from 0.1 to 1
- halting: int32 [16384], P(('dp', 'expert')), may hold values 0 or 1
- head_routes: int32 [16384, 4], P(('dp', 'expert')), may hold values from 0 to 23, all different within a row
- expert_routes: int32 [16384, 2], P(('dp', 'expert')), may hold values from 0 to 15, all different within a row; in each aligned block of 512 rows (0 to 511, 512 to 1023, ...) at most 128 rows name the same one
- first_gain: bfloat16 [512], replicated, may hold values from 0.25 to 1.75
- first_bias: bfloat16 [512], replicated, may hold values from -4 to 4
- query_weight: bfloat16 [512, 1536], replicated, may hold values from -0.5 to 0.5
- key_weight: bfloat16 [512, 64], replicated, may hold values from -0.25 to 0.25
- value_weight: bfloat16 [512, 64], replicated, may hold values from -0.25 to 0.25
- output_weight: bfloat16 [1536, 512], replicated, may hold values from -4 to 4
- head_router: bfloat16 [512, 24], replicated, may hold values from -0.125 to 0.125
- second_gain: bfloat16 [512], replicated, may hold values from 0.25 to 1.75
- second_bias: bfloat16 [512], replicated, may hold values from -4 to 4
- expert_router: bfloat16 [512, 16], replicated, may hold values from -0.1875 to 0.1875
- expert_in: bfloat16 [16, 512, 2048], P('expert'), may hold values from -0.25 to 0.25
- expert_out: bfloat16 [16, 2048, 512], P('expert'), may hold values from -0.1875 to 0.1875
- halt_weight: bfloat16 [512], replicated, may hold values from -0.25 to 0.25
- state_cotan: bfloat16 [16384, 512], P(('dp', 'expert')), may hold values from -6 to 6
- accum_cotan: bfloat16 [16384, 512], P(('dp', 'expert')), may hold values from -6 to 6
- remain_cotan: float32 [16384], P(('dp', 'expert')), may hold values from -6 to 6
Outputs:
- new_state: bfloat16 [16384, 512], P(('dp', 'expert'))
- accum_part: float32 [16384, 512], P(('dp', 'expert'))
- remain_left: float32 [16384], P(('dp', 'expert'))
- tokens_grad: float32 [16384, 512], P(('dp', 'expert'))
- remain_grad: float32 [16384], P(('dp', 'expert'))
- first_gain_grad: float32 [512], replicated
- first_bias_grad: float32 [512], replicated
- query_grad: float32 [512, 1536], replicated
- key_grad: float32 [512, 64], replicated
- value_grad: float32 [512, 64], replicated
- output_grad: float32 [1536, 512], replicated
- head_router_grad: float32 [512, 24], replicated
- second_gain_grad: float32 [512], replicated
- second_bias_grad: float32 [512], replicated
- expert_router_grad: float32 [512, 16], replicated
- expert_in_grad: float32 [16, 512, 2048], P('expert', None, 'dp')
- expert_out_grad: float32 [16, 2048, 512], P('expert', 'dp')
- halt_grad: float32 [512], replicated
Inputs may be any that keep to these rules, and one draw needn't show every extreme that they name: `head_routes`: each row names 4 different head experts. `expert_routes`: each row names 2 different FFN experts; among the 512 rows of one device no expert is named by more than 128 rows.
All inputs are finite; a program needn't handle non-finite values. No bound on the sum of `halting` on one device may be relied on, other than what follows from the above.
Results may differ from a plain program's by a relative error of at most 0.019.
Values may be sent and summed in bfloat16 or wider, within the bound.
A program may use at most 128 MiB of HBM per device.

v0:
```python
import math

import jax
import jax.numpy as jnp
from jax import lax
from jax.sharding import PartitionSpec as P

epsilon = 1e-05
highest = lax.Precision.HIGHEST


def norm_forward(values, scales, offset):
    centre = jnp.mean(values, axis=-1, keepdims=True)
    shifted = values - centre
    spread = jnp.mean(shifted * shifted, axis=-1, keepdims=True)
    inverse = lax.rsqrt(spread + epsilon)
    normal = shifted * inverse
    return (normal * scales + offset, normal, inverse)


def norm_backward(upstream, normal, inverse, scales):
    scaled = upstream * scales
    inner_sum = (
        scaled
        - jnp.mean(scaled, axis=-1, keepdims=True)
        - normal * jnp.mean(scaled * normal, axis=-1, keepdims=True)
    )
    return (inner_sum * inverse, jnp.sum(upstream * normal, axis=0), jnp.sum(upstream, axis=0))


def gelu_slope(pre_act):
    cumulative = 0.5 * (1.0 + lax.erf(pre_act * (1.0 / math.sqrt(2.0))))
    density = jnp.exp(-0.5 * pre_act * pre_act) * (1.0 / math.sqrt(2.0 * math.pi))
    return cumulative + pre_act * density


def slot_targets(routes, experts, room_rows):
    flattened = routes.reshape(-1)
    hot_rows = (flattened[:, None] == jnp.arange(experts, dtype=jnp.int32)[None, :]).astype(
        jnp.int32
    )
    before = jnp.cumsum(hot_rows, axis=0) - hot_rows
    return flattened * room_rows + jnp.sum(hot_rows * before, axis=1)


def matmul_nt(left, right):
    return lax.dot_general(
        left, right, (((1,), (1,)), ((), ())), preferred_element_type=jnp.float32
    )


def matmul_tn(left, right):
    return lax.dot_general(
        left, right, (((0,), (0,)), ((), ())), preferred_element_type=jnp.float32
    )


def masked_scores(flat_query, key_rows, top_att, scaling):
    scores = matmul_nt(flat_query, key_rows) * scaling
    row_pos = lax.broadcasted_iota(jnp.int32, scores.shape, 0) // top_att
    col_pos = lax.broadcasted_iota(jnp.int32, scores.shape, 1)
    return jnp.where(col_pos <= row_pos, scores, jnp.float32(-1e30))


def attend(query_sel, key_rows, value_rows, scaling):
    tok_rows, top_att, head_size = query_sel.shape
    flat_query = query_sel.reshape(tok_rows * top_att, head_size)
    scores = masked_scores(flat_query, key_rows, top_att, scaling)
    row_peak = jnp.max(scores, axis=1, keepdims=True)
    raised = jnp.exp(scores - row_peak)
    denom_sum = jnp.sum(raised, axis=1, keepdims=True)
    attn_prob = (raised / denom_sum).astype(jnp.bfloat16)
    output = jnp.dot(attn_prob, value_rows, preferred_element_type=jnp.float32)
    return (output.reshape(tok_rows, top_att, head_size), row_peak + jnp.log(denom_sum))


def attend_back(query_sel, key_rows, value_rows, log_total, grad_heads, scaling):
    tok_rows, top_att, head_size = query_sel.shape
    flat_query = query_sel.reshape(tok_rows * top_att, head_size)
    flat_grad = grad_heads.reshape(tok_rows * top_att, head_size)
    scores = masked_scores(flat_query, key_rows, top_att, scaling)
    attn_prob = jnp.exp(scores - log_total)
    grad_prob = matmul_nt(flat_grad, value_rows)
    grad_values = matmul_tn(attn_prob.astype(jnp.bfloat16), flat_grad)
    row_inner = jnp.sum(attn_prob * grad_prob, axis=1, keepdims=True)
    grad_scores = (attn_prob * (grad_prob - row_inner)).astype(jnp.bfloat16)
    grad_query = jnp.dot(grad_scores, key_rows, preferred_element_type=jnp.float32) * scaling
    grad_keys = matmul_tn(grad_scores, flat_query) * scaling
    return (grad_query.reshape(tok_rows, top_att, head_size), grad_keys, grad_values)


def body(
    tokens,
    remain,
    halting,
    head_routes,
    expert_routes,
    first_gain,
    first_bias,
    query_weight,
    key_weight,
    value_weight,
    output_weight,
    head_router,
    second_gain,
    second_bias,
    expert_router,
    expert_in,
    expert_out,
    halt_weight,
    state_cotan,
    accum_cotan,
    remain_cotan,
):
    tok_rows, model_width = tokens.shape
    head_size = key_weight.shape[1]
    num_heads = query_weight.shape[1] // head_size
    top_ffn = expert_routes.shape[1]
    local_exp = expert_in.shape[0]
    experts_all = local_exp * lax.axis_size("expert")
    capacity = 4 * tok_rows // experts_all
    scaling = head_size ** (-0.5)
    inputs = tokens.astype(jnp.float32)
    active = halting.astype(jnp.float32)
    gain_one = first_gain.astype(jnp.float32)
    gain_two = second_gain.astype(jnp.float32)
    normed_one, normal_one, inverse_one = norm_forward(
        inputs, gain_one, first_bias.astype(jnp.float32)
    )
    attn_in = normed_one.astype(jnp.bfloat16)
    query_all = jnp.dot(attn_in, query_weight, preferred_element_type=jnp.float32).reshape(
        tok_rows, num_heads, head_size
    )
    head_hot = (
        head_routes[:, :, None] == jnp.arange(num_heads, dtype=jnp.int32)[None, None, :]
    ).astype(jnp.float32)
    query_sel = jnp.einsum("teh,tae->tah", query_all, head_hot, precision=highest).astype(
        jnp.bfloat16
    )
    key_rows = jnp.dot(attn_in, key_weight, preferred_element_type=jnp.float32).astype(jnp.bfloat16)
    value_rows = jnp.dot(attn_in, value_weight, preferred_element_type=jnp.float32).astype(
        jnp.bfloat16
    )
    head_logits = jnp.dot(attn_in, head_router, preferred_element_type=jnp.float32)
    head_gate = jax.nn.softmax(jnp.take_along_axis(head_logits, head_routes, axis=1), axis=1)
    heads_out, log_total = attend(query_sel, key_rows, value_rows, scaling)
    weighted = (head_gate[:, :, None] * heads_out).astype(jnp.bfloat16)
    head_hot_low = head_hot.astype(jnp.bfloat16)
    spread_out = (
        jnp.einsum("tah,tae->teh", weighted, head_hot_low, preferred_element_type=jnp.float32)
        .astype(jnp.bfloat16)
        .reshape(tok_rows, num_heads * head_size)
    )
    hidden_one = inputs + jnp.dot(spread_out, output_weight, preferred_element_type=jnp.float32)
    normed_two, normal_two, inverse_two = norm_forward(
        hidden_one, gain_two, second_bias.astype(jnp.float32)
    )
    ffn_in = normed_two.astype(jnp.bfloat16)
    expert_logits = jnp.dot(ffn_in, expert_router, preferred_element_type=jnp.float32)
    expert_gate = jax.nn.softmax(jnp.take_along_axis(expert_logits, expert_routes, axis=1), axis=1)
    targets = slot_targets(expert_routes, experts_all, capacity)
    outgoing = (
        jnp.zeros((experts_all * capacity, model_width), jnp.bfloat16)
        .at[targets]
        .set(jnp.repeat(ffn_in, top_ffn, axis=0))
    )
    arrived = lax.all_to_all(
        outgoing.reshape(experts_all, capacity, model_width),
        "expert",
        split_axis=0,
        concat_axis=1,
        tiled=True,
    )
    pre_act = jnp.einsum("erd,edf->erf", arrived, expert_in, preferred_element_type=jnp.float32)
    inner_act = jax.nn.gelu(pre_act, approximate=False).astype(jnp.bfloat16)
    produced = jnp.einsum(
        "erf,efd->erd", inner_act, expert_out, preferred_element_type=jnp.float32
    ).astype(jnp.bfloat16)
    returned = lax.all_to_all(produced, "expert", split_axis=1, concat_axis=0, tiled=True).reshape(
        experts_all * capacity, model_width
    )
    picked = returned[targets].astype(jnp.float32).reshape(tok_rows, top_ffn, model_width)
    hidden = hidden_one + jnp.sum(expert_gate[:, :, None] * picked, axis=1)
    halt_vector = halt_weight.astype(jnp.float32)
    halt_prob = jax.nn.sigmoid(jnp.dot(hidden, halt_vector, precision=highest))
    halt_share = active * remain * halt_prob
    new_state = jnp.where(active[:, None] > 0.5, hidden, inputs).astype(jnp.bfloat16)
    accum_part = halt_share[:, None] * hidden
    remain_left = remain * (1.0 - active * halt_prob)
    grad_state = state_cotan.astype(jnp.float32)
    grad_accum = accum_cotan.astype(jnp.float32)
    grad_share = jnp.sum(grad_accum * hidden, axis=1)
    grad_logit = active * remain * (grad_share - remain_cotan) * halt_prob * (1.0 - halt_prob)
    remain_grad = active * halt_prob * grad_share + (1.0 - active * halt_prob) * remain_cotan
    grad_hidden = (
        active[:, None] * grad_state
        + halt_share[:, None] * grad_accum
        + grad_logit[:, None] * halt_vector[None, :]
    )
    halt_sum = jnp.dot(grad_logit, hidden, precision=highest)
    grad_gate = jnp.sum(grad_hidden[:, None, :] * picked, axis=2)
    grad_esel = expert_gate * (grad_gate - jnp.sum(expert_gate * grad_gate, axis=1, keepdims=True))
    expert_hot = (
        expert_routes[:, :, None] == jnp.arange(experts_all, dtype=jnp.int32)[None, None, :]
    ).astype(jnp.float32)
    grad_elogits = jnp.einsum("tk,tke->te", grad_esel, expert_hot, precision=highest)
    grad_prod = (
        (expert_gate[:, :, None] * grad_hidden[:, None, :])
        .astype(jnp.bfloat16)
        .reshape(tok_rows * top_ffn, model_width)
    )
    grad_out_rows = (
        jnp.zeros((experts_all * capacity, model_width), jnp.bfloat16).at[targets].set(grad_prod)
    )
    grad_arrived = lax.all_to_all(
        grad_out_rows.reshape(experts_all, capacity, model_width),
        "expert",
        split_axis=0,
        concat_axis=1,
        tiled=True,
    )
    grad_inner = jnp.einsum(
        "erd,efd->erf", grad_arrived, expert_out, preferred_element_type=jnp.float32
    )
    grad_pre = (grad_inner * gelu_slope(pre_act)).astype(jnp.bfloat16)
    grad_rows = jnp.einsum(
        "erf,edf->erd", grad_pre, expert_in, preferred_element_type=jnp.float32
    ).astype(jnp.bfloat16)
    grad_back = lax.all_to_all(
        grad_rows, "expert", split_axis=1, concat_axis=0, tiled=True
    ).reshape(experts_all * capacity, model_width)
    in_terms = jnp.einsum("erd,erf->edf", arrived, grad_pre, preferred_element_type=jnp.float32)
    out_terms = jnp.einsum(
        "erf,erd->efd", inner_act, grad_arrived, preferred_element_type=jnp.float32
    )
    expert_in_grad, expert_out_grad = (
        lax.psum_scatter(
            in_terms.astype(jnp.bfloat16), "dp", scatter_dimension=2, tiled=True
        ).astype(jnp.float32),
        lax.psum_scatter(
            out_terms.astype(jnp.bfloat16), "dp", scatter_dimension=1, tiled=True
        ).astype(jnp.float32),
    )
    grad_ffn_in = jnp.sum(
        grad_back[targets].astype(jnp.float32).reshape(tok_rows, top_ffn, model_width), axis=1
    )
    grad_ffn_in = grad_ffn_in + matmul_nt(grad_elogits, expert_router.astype(jnp.float32))
    router_two_sum = matmul_tn(ffn_in.astype(jnp.float32), grad_elogits)
    norm_two_in, gain_two_sum, bias_two_sum = norm_backward(
        grad_ffn_in, normal_two, inverse_two, gain_two
    )
    grad_one = grad_hidden + norm_two_in
    grad_attn = grad_one.astype(jnp.bfloat16)
    output_sum = matmul_tn(spread_out, grad_attn)
    grad_spread = matmul_nt(grad_attn, output_weight).reshape(tok_rows, num_heads, head_size)
    grad_weighted = jnp.einsum("teh,tae->tah", grad_spread, head_hot, precision=highest)
    grad_hgate = jnp.sum(grad_weighted * heads_out, axis=2)
    grad_heads = (head_gate[:, :, None] * grad_weighted).astype(jnp.bfloat16)
    grad_query, grad_keys, grad_values = attend_back(
        query_sel, key_rows, value_rows, log_total, grad_heads, scaling
    )
    grad_query = grad_query.astype(jnp.bfloat16)
    grad_qall = (
        jnp.einsum("tah,tae->teh", grad_query, head_hot_low, preferred_element_type=jnp.float32)
        .astype(jnp.bfloat16)
        .reshape(tok_rows, num_heads * head_size)
    )
    grad_keys = grad_keys.astype(jnp.bfloat16)
    grad_values = grad_values.astype(jnp.bfloat16)
    grad_hsel = head_gate * (grad_hgate - jnp.sum(head_gate * grad_hgate, axis=1, keepdims=True))
    grad_hlogits = jnp.einsum("ta,tae->te", grad_hsel, head_hot, precision=highest)
    grad_ain = (
        matmul_nt(grad_qall, query_weight)
        + matmul_nt(grad_keys, key_weight)
        + matmul_nt(grad_values, value_weight)
    )
    grad_ain = grad_ain + matmul_nt(grad_hlogits, head_router.astype(jnp.float32))
    query_sum = matmul_tn(attn_in, grad_qall)
    key_sum = matmul_tn(attn_in, grad_keys)
    value_sum = matmul_tn(attn_in, grad_values)
    router_one_sum = matmul_tn(attn_in.astype(jnp.float32), grad_hlogits)
    norm_one_in, gain_one_sum, bias_one_sum = norm_backward(
        grad_ain, normal_one, inverse_one, gain_one
    )
    tokens_grad = grad_one + norm_one_in + (1.0 - active)[:, None] * grad_state
    totals = lax.psum(
        (
            gain_one_sum,
            bias_one_sum,
            query_sum,
            key_sum,
            value_sum,
            output_sum,
            router_one_sum,
            gain_two_sum,
            bias_two_sum,
            router_two_sum,
            halt_sum,
        ),
        ("dp", "expert"),
    )
    return (
        new_state,
        accum_part,
        remain_left,
        tokens_grad,
        remain_grad,
        totals[0],
        totals[1],
        totals[2],
        totals[3],
        totals[4],
        totals[5],
        totals[6],
        totals[7],
        totals[8],
        totals[9],
        expert_in_grad,
        expert_out_grad,
        totals[10],
    )


def solution(mesh):
    in_specs = (
        P(("dp", "expert"), None),
        P(("dp", "expert")),
        P(("dp", "expert")),
        P(("dp", "expert"), None),
        P(("dp", "expert"), None),
        P(),
        P(),
        P(),
        P(),
        P(),
        P(),
        P(),
        P(),
        P(),
        P(),
        P("expert", None, None),
        P("expert", None, None),
        P(),
        P(("dp", "expert"), None),
        P(("dp", "expert"), None),
        P(("dp", "expert")),
    )
    out_specs = (
        P(("dp", "expert"), None),
        P(("dp", "expert"), None),
        P(("dp", "expert")),
        P(("dp", "expert"), None),
        P(("dp", "expert")),
        P(),
        P(),
        P(),
        P(),
        P(),
        P(),
        P(),
        P(),
        P(),
        P(),
        P("expert", None, "dp"),
        P("expert", "dp", None),
        P(),
    )
    return jax.shard_map(body, mesh=mesh, in_specs=in_specs, out_specs=out_specs, check_vma=False)
```

profile of v0, /device:TPU:0, one launch (start us, length us, event | category | flops | bytes accessed | tf_op | source)
XLA Modules:
  0.0 831.9 jit_solution(2302333131944766409)
XLA Ops:
  15.4 16.8 %gather_fusion.2 = f32[2048]{0:T(1024)S(1)} fusion(f32[512,24]{0,1:T(8,128)S(1)} %fusion.84, s32[2048]{0:T(1024)S(1)} %reshape.304), kind=kCustom, calls=%fused_computation.2 | custom fusion | bytes 32768 | tf_op jit(solution)/shard_map/jit(take_along_axis)/gather | solution.py:145
  37.1 5.9 copy.219
  44.3 5.4 convolution_convert_fusion.6
  54.6 4.7 online-softmax
  59.3 5.8 convolution_convert_fusion.3
  65.1 5.2 copy.222
  77.8 4.5 reduce-window.6
  83.1 7.2 scatter_custom_fusion
  90.3 55.7 %all_to_all.66 = bf16[16,128,512]{2,1,0:T(8,128)(2,1)S(1)} all-to-all(bf16[16,128,512]{2,1,0:T(8,128)(2,1)} %bitcast.135), channel_id=1, replica_groups=mesh['dp'=4,'expert'=8] {'expert'}, dimensions={0} | all-to-all | bytes 4194304 | tf_op jit(solution)/shard_map/all_to_all | solution.py:167
  147.5 17.2 %fusion.16 = (u8[1024,2048]{1,0:T(8,128)(4,1)S(1)}, u8[1024,2048]{1,0:T(8,128)(4,1)}, f32[2,1024,2048]{2,1,0:T(8,128)}) fusion(bf16[2,1024,512]{2,1,0:T(8,128)(2,1)} %bitcast.144, bf16[2,512,2048]{2,1,0:T(8,128)(2,1)} %param.36), kind=kOutput, calls=%fused_computation.42 | convolution fusion | flops 4345298944 | bytes 27262976 | tf_op jit(solution)/shard_map/erd,edf->erf/dot_general | solution.py:174
  164.6 40.0 %fusion.2 = bf16[2,1024,2048]{2,1,0:T(8,128)(2,1)S(1)} fusion(f32[2,1024,2048]{2,1,0:T(8,128)} %get-tuple-element.146, u8[1024,2048]{1,0:T(8,128)(4,1)} %get-tuple-element.109, u8[1024,2048]{1,0:T(8,128)(4,1)S(1)} %get-tuple-element.108), kind=kLoop, calls=%fused_computation.10 | loop fusion | flops 293601280 | bytes 29360128 | tf_op jit(solution)/shard_map/convert_element_type | solution.py:175
  204.7 4.7 convolution_convert_fusion.5
  212.9 4.4 all-to-all-start.1
  217.9 8.8 %gather_fusion.3 = f32[1024]{0:T(1024)S(1)} fusion(f32[512,16]{0,1:T(8,128)S(1)} %fusion.95, s32[1024]{0:T(1024)S(1)} %reshape.310), kind=kCustom, calls=%fused_computation.3 | custom fusion | bytes 16384 | tf_op jit(solution)/shard_map/jit(take_along_axis)/gather | solution.py:160
  230.5 34.1 %all-to-all-done.1 = bf16[2,1024,512]{2,0,1:T(2,128)(2,1)} async-done(((bf16[2,1024,512]{2,0,1:T(2,128)(2,1)}), bf16[2,1024,512]{2,0,1:T(2,128)(2,1)}, u32[]{:S(2)}, u32[]{:S(2)}) %all-to-all-start.1) | async-done | bytes 2097184 | tf_op jit(solution)/shard_map/all_to_all | solution.py:179
  267.9 5.8 gather_fusion
  276.1 4.4 multiply_reduce_fusion.2
  296.0 7.7 scatter_custom_fusion.1
  303.8 52.4 %all_to_all.67 = bf16[16,128,512]{2,1,0:T(8,128)(2,1)S(1)} all-to-all(bf16[16,128,512]{2,1,0:T(8,128)(2,1)} %bitcast.134), channel_id=1, replica_groups=mesh['dp'=4,'expert'=8] {'expert'}, dimensions={0} | all-to-all | bytes 4194304 | tf_op jit(solution)/shard_map/all_to_all | solution.py:215
  357.7 11.6 %convolution_convert_fusion = bf16[2,2048,512]{2,1,0:T(8,128)(2,1)} fusion(bf16[2,1024,2048]{2,1,0:T(8,128)(2,1)} %copy-done.15, bf16[2,1024,512]{2,1,0:T(8,128)(2,1)S(1)} %bitcast.146), kind=kOutput, calls=%fused_computation.43 | convolution fusion | flops 4297064448 | bytes 14680064 | tf_op jit(solution)/shard_map/erf,erd->efd/dot_general | solution.py:233
  369.3 13.7 %fusion.8 = bf16[2,1024,2048]{2,1,0:T(8,128)(2,1)S(1)} fusion(f32[2,1024,2048]{2,1,0:T(8,128)} %get-tuple-element.146, bf16[2,1024,512]{2,1,0:T(8,128)(2,1)} %bitcast.147, bf16[2,2048,512]{2,1,0:T(8,128)(2,1)} %param.37), kind=kOutput, calls=%fused_computation.16 | convolution fusion | flops 4336910336 | bytes 31457280 | tf_op jit(solution)/shard_map/erd,efd->erf/dot_general | solution.py:222
  383.0 4.8 convolution_convert_fusion.4
  400.8 10.7 %convolution_convert_fusion.1 = bf16[2,512,2048]{2,1,0:T(8,128)(2,1)} fusion(bf16[2,1024,512]{2,1,0:T(8,128)(2,1)} %bitcast.145, bf16[2,1024,2048]{2,1,0:T(8,128)(2,1)} %copy-done.83), kind=kOutput, calls=%fused_computation.44 | convolution fusion | flops 4297064448 | bytes 14680064 | tf_op jit(solution)/shard_map/erd,erf->edf/dot_general | solution.py:232
  417.9 25.3 %all-to-all-done.3 = bf16[2,1024,512]{2,0,1:T(2,128)(2,1)} async-done(((bf16[2,1024,512]{2,0,1:T(2,128)(2,1)}), bf16[2,1024,512]{2,0,1:T(2,128)(2,1)}, u32[]{:S(2)}, u32[]{:S(2)}) %all-to-all-start.3) | async-done | bytes 2097184 | tf_op jit(solution)/shard_map/all_to_all | solution.py:229
  446.5 7.2 gather_fusion.1
  457.1 5.1 reduce_sum.229
  472.1 5.9 copy.249
  478.1 6.8 multiply_convert_fusion.3
  490.2 5.5 convolution_convert_fusion.2
  495.7 4.9 copy.253
  536.3 108.9 %all-reduce.5.cloned.1.call-done = (f32[512]{0:T(512)}, f32[512]{0:T(512)}, f32[512,24]{0,1:T(8,128)}, f32[512]{0:T(512)}, f32[512]{0:T(512)}, /*index=5*/f32[512,16]{0,1:T(8,128)}, f32[512]{0:T(512)}) async-done(((f32[512]{0:T(512)}, f32[512]{0:T(512)}, f32[512,24]{0,1:T(8,128)}, f32[512]{0:T(512)}, f32[512]{0:T(512)}, /*index=5*/f32[512,16]{0,1:T(8,128)}, f32[512]{0:T(512)}), (f32[512]{0:T(512)}, ...) | async-done | bytes 92176 | tf_op jit(solution)/shard_map/psum | solution.py:286
  645.2 166.4 %all-reduce.7.cloned.1.call-done = (f32[512,1536]{1,0:T(8,128)}, f32[512,64]{0,1:T(8,128)}, f32[512,64]{0,1:T(8,128)}, f32[1536,512]{1,0:T(8,128)}) async-done(((f32[512,1536]{1,0:T(8,128)}, f32[512,64]{0,1:T(8,128)}, f32[512,64]{0,1:T(8,128)}, f32[1536,512]{1,0:T(8,128)}), (f32[512,1536]{1,0:T(8,128)}, f32[512,64]{0,1:T(8,128)}, f32[512,64]{0,1:T(8,128)}, ...) | async-done | bytes 6553616 | tf_op jit(solution)/shard_map/psum | solution.py:286
  (320 shorter events, 147.4 us)
Async XLA Ops:
  8.0 62.3 %copy-start = (bf16[1536,512]{1,0:T(8,128)(2,1)S(1)}, bf16[1536,512]{1,0:T(8,128)(2,1)}, u32[]{:S(2)}) copy-start(bf16[1536,512]{1,0:T(8,128)(2,1)} %param.31) | copy-start | bytes 4718596
  9.7 49.6 %copy-start.21 = (s32[512,4]{1,0:T(8,128)}, s32[512,4]{1,0:T(8,128)S(1)}, u32[]{:S(2)}) copy-start(s32[512,4]{1,0:T(8,128)S(1)} %copy.214) | copy-start | bytes 24580
  12.9 57.4 %copy-start.5 = (bf16[512,512]{0,1:T(8,128)(2,1)}, bf16[512,512]{0,1:T(8,128)(2,1)S(1)}, u32[]{:S(2)}) copy-start(bf16[512,512]{0,1:T(8,128)(2,1)S(1)} %copy.213) | copy-start | bytes 1572868
  15.2 28.0 %copy-start.2 = (bf16[512,512]{0,1:T(8,128)(2,1)}, bf16[512,512]{0,1:T(8,128)(2,1)S(1)}, u32[]{:S(2)}) copy-start(bf16[512,512]{0,1:T(8,128)(2,1)S(1)} %fusion.34) | copy-start | bytes 1572868
  15.4 17.2 %copy-start.49 = (s32[512,4]{0,1:T(4,128)S(1)}, s32[512,4]{0,1:T(4,128)}, u32[]{:S(2)}) copy-start(s32[512,4]{0,1:T(4,128)} %param.24) | copy-start | bytes 24580
  32.6 10.4 %copy-start.43 = (f32[512,4]{0,1:T(4,128)}, f32[512,4]{0,1:T(4,128)S(1)}, u32[]{:S(2)}) copy-start(f32[512,4]{0,1:T(4,128)S(1)} %get-tuple-element.134) | copy-start | bytes 24580
  32.6 10.4 %copy-start.57 = (f32[512]{0:T(512)}, f32[512]{0:T(512)S(1)}, u32[]{:S(2)}) copy-start(f32[512]{0:T(512)S(1)} %get-tuple-element.133) | copy-start | bytes 6148
  32.7 10.3 %copy-start.70 = (f32[512]{0:T(512)}, f32[512]{0:T(512)S(1)}, u32[]{:S(2)}) copy-start(f32[512]{0:T(512)S(1)} %fusion.77) | copy-start | bytes 6148
  32.8 26.5 %copy-start.33 = (f32[512,4]{1,0:T(8,128)}, f32[512,4]{1,0:T(8,128)S(1)}, u32[]{:S(2)}) copy-start(f32[512,4]{1,0:T(8,128)S(1)} %copy.217) | copy-start | bytes 24580
  43.2 11.4 %copy-start.40 = (bf16[512,64]{0,1:T(8,128)(2,1)}, bf16[512,64]{0,1:T(8,128)(2,1)S(1)}, u32[]{:S(2)}) copy-start(bf16[512,64]{0,1:T(8,128)(2,1)S(1)} %convolution_convert_fusion.7) | copy-start | bytes 196612
  43.4 11.2 %copy-start.29 = (f32[512,64]{0,1:T(8,128)}, f32[512,64]{0,1:T(8,128)S(1)}, u32[]{:S(2)}) copy-start(f32[512,64]{0,1:T(8,128)S(1)} %fusion.94) | copy-start | bytes 393220
  164.6 40.0 %copy-start.81 = (bf16[2,2048,512]{2,1,0:T(8,128)(2,1)S(1)}, bf16[2,2048,512]{2,1,0:T(8,128)(2,1)}, u32[]{:S(2)}) copy-start(bf16[2,2048,512]{2,1,0:T(8,128)(2,1)} %param.37) | copy-start | bytes 12582916
  209.4 8.3 copy-start.50
  212.9 51.7 %all-to-all-start.1 = ((bf16[2,1024,512]{2,0,1:T(2,128)(2,1)}), bf16[2,1024,512]{2,0,1:T(2,128)(2,1)}, u32[]{:S(2)}, u32[]{:S(2)}) async-start(bf16[2,1024,512]{2,0,1:T(2,128)(2,1)} %copy.233), calls=%async_computation.1 | async-start | bytes 4194304 | tf_op jit(solution)/shard_map/all_to_all | solution.py:179
  217.3 313.4 %reduce-scatter.5.cloned.1.call-start = ((), (), s32[]{:S(2)}) async-start(), calls=%async_computation.7 | async-start | bytes 5242880 | tf_op jit(solution)/shard_map/reduce_scatter | solution.py:240
  217.9 9.4 %copy-start.35 = (bf16[512,512]{1,0:T(8,128)(2,1)S(1)}, bf16[512,512]{1,0:T(8,128)(2,1)}, u32[]{:S(2)}) copy-start(bf16[512,512]{1,0:T(8,128)(2,1)} %param.40) | copy-start | bytes 1572868
  217.9 12.5 %copy-start.72 = (s32[512]{0:T(512)S(1)}, s32[512]{0:T(512)}, u32[]{:S(2)}) copy-start(s32[512]{0:T(512)} %param.23) | copy-start | bytes 6148
  369.3 13.7 %copy-start.82 = (bf16[2,512,2048]{2,1,0:T(8,128)(2,1)S(1)}, bf16[2,512,2048]{2,1,0:T(8,128)(2,1)}, u32[]{:S(2)}) copy-start(bf16[2,512,2048]{2,1,0:T(8,128)(2,1)} %param.36) | copy-start | bytes 12582916
  387.8 8.1 copy-start.68
  391.3 51.9 %all-to-all-start.3 = ((bf16[2,1024,512]{2,0,1:T(2,128)(2,1)}), bf16[2,1024,512]{2,0,1:T(2,128)(2,1)}, u32[]{:S(2)}, u32[]{:S(2)}) async-start(bf16[2,1024,512]{2,0,1:T(2,128)(2,1)} %copy.241), calls=%async_computation.3 | async-start | bytes 4194304 | tf_op jit(solution)/shard_map/all_to_all | solution.py:229
  395.7 137.8 %reduce-scatter.3.cloned.1.call-start = ((), (), s32[]{:S(2)}) async-start(), calls=%async_computation.6 | async-start | bytes 5242880 | tf_op jit(solution)/shard_map/reduce_scatter | solution.py:237
  411.4 233.8 %all-reduce.5.cloned.1.call-start = ((), (), s32[]{:S(2)}) async-start(), calls=%async_computation.8 | async-start | bytes 184320 | tf_op jit(solution)/shard_map/psum | solution.py:286
  453.7 11.0 %copy-start.32 = (f32[512,1,16]{2,1,0:T(1,128)S(1)}, f32[512,1,16]{2,1,0:T(1,128)}, u32[]{:S(2)}) copy-start(f32[512,1,16]{2,1,0:T(1,128)} %copy-done.31) | copy-start | bytes 98308
  453.7 11.0 %copy-start.51 = (bf16[512,16]{0,1:T(8,128)(2,1)S(1)}, bf16[512,16]{0,1:T(8,128)(2,1)}, u32[]{:S(2)}) copy-start(bf16[512,16]{0,1:T(8,128)(2,1)} %param.35) | copy-start | bytes 49156
  453.7 11.0 %copy-start.56 = (f32[512]{0:T(512)S(1)}, f32[512]{0:T(512)}, u32[]{:S(2)}) copy-start(f32[512]{0:T(512)} %copy-done.55) | copy-start | bytes 6148
  453.7 11.0 %copy-start.65 = (f32[512]{0:T(512)S(1)}, f32[512]{0:T(512)}, u32[]{:S(2)}) copy-start(f32[512]{0:T(512)} %copy-done.64) | copy-start | bytes 6148
  453.7 11.0 %copy-start.67 = (f32[512]{0:T(512)S(1)}, f32[512]{0:T(512)}, u32[]{:S(2)}) copy-start(f32[512]{0:T(512)} %copy-done.66) | copy-start | bytes 6148
  490.2 11.5 %copy-start.44 = (f32[512,4]{0,1:T(4,128)S(1)}, f32[512,4]{0,1:T(4,128)}, u32[]{:S(2)}) copy-start(f32[512,4]{0,1:T(4,128)} %copy-done.43) | copy-start | bytes 24580
  490.2 11.5 %copy-start.58 = (f32[512]{0:T(512)S(1)}, f32[512]{0:T(512)}, u32[]{:S(2)}) copy-start(f32[512]{0:T(512)} %copy-done.57) | copy-start | bytes 6148
  490.2 11.6 %copy-start.71 = (f32[512]{0:T(512)S(1)}, f32[512]{0:T(512)}, u32[]{:S(2)}) copy-start(f32[512]{0:T(512)} %copy-done.70) | copy-start | bytes 6148
  495.7 10.1 %copy-start.3 = (bf16[512,512]{0,1:T(8,128)(2,1)S(1)}, bf16[512,512]{0,1:T(8,128)(2,1)}, u32[]{:S(2)}) copy-start(bf16[512,512]{0,1:T(8,128)(2,1)} %copy-done.2) | copy-start | bytes 1572868
  520.6 291.1 %all-reduce.7.cloned.1.call-start = ((), (), s32[]{:S(2)}) async-start(), calls=%async_computation.9 | async-start | bytes 13107200 | tf_op jit(solution)/shard_map/psum | solution.py:286
  (58 other events, 216.2 us)
Sparse Core Ops, SparseCore 0:
  369.4 43.6 reduce-scatter.4
  415.7 44.3 reduce-scatter.2
Sparse Core Ops, SparseCore 1:
  520.7 124.5 all-reduce.4
  652.4 159.2 all-reduce.6
where the time goes:
time: 841 us; the launch traced here: 832 us
  waiting for transfers between devices  335 us (40%)
  local copies, waits for them, and re-layouts  142 us (17%)
  matrix products  129 us (15%)
  blocking collectives  108 us (13%)
  other arithmetic  86.6 us (10%)
  between operations  17.2 us (2%)
  starting transfers between devices  9.08 us (1%)
    psum x2, waiting for transfers between devices, body(): lax.psum((gain_one_sum, bias_one_sum, query_sum, key_sum, value_sum, outp...  275 us
    all_to_all x1, blocking collectives, body(): lax.all_to_all(outgoing.reshape(experts_all, capacity, model_width), 'exp...  55.7 us
    all_to_all x1, blocking collectives, body(): lax.all_to_all(grad_out_rows.reshape(experts_all, capacity, model_width),...  52.4 us
    convert_element_type x1, other arithmetic, body(): inner_act = jax.nn.gelu(pre_act, approximate=False).astype(jnp.bfloat16)  40 us
    all_to_all x1, waiting for transfers between devices, body(): lax.all_to_all(produced, 'expert', split_axis=1, concat_axis=0, tiled=True)  34.1 us
    unnamed x188, local copies, waits for them, and re-layouts  28.8 us
    all_to_all x1, waiting for transfers between devices, body(): lax.all_to_all(grad_rows, 'expert', split_axis=1, concat_axis=0, tiled=True)  25.3 us
    gather x5, local copies, waits for them, and re-layouts, body(): jnp.take_along_axis(head_logits, head_routes, axis=1)  17.5 us
  transfers between devices with their start and end apart: 6, of which 4 were waited for; matrix products, arithmetic and copies ran while one was open for 18% of the time, Pallas kernels for 0%

commit v1 on v0

v1 whole, which is shorter than its diff:
```python
import functools
import math

import jax
import jax.numpy as jnp
from jax import lax
from jax.experimental import pallas as pl
from jax.experimental.pallas import tpu as pltpu
from jax.sharding import PartitionSpec as P

epsilon = 1e-05
f32 = jnp.float32
bf16 = jnp.bfloat16
MESH = pl.DeviceIdType.MESH
VMEM_LIMIT = 67043328


def dot_nn(left, right):
    return jnp.dot(left, right, preferred_element_type=f32)


def dot_nt(left, right):
    return lax.dot_general(left, right, (((1,), (1,)), ((), ())), preferred_element_type=f32)


def dot_tn(left, right):
    return lax.dot_general(left, right, (((0,), (0,)), ((), ())), preferred_element_type=f32)


def iota(shape, axis):
    return lax.broadcasted_iota(jnp.int32, shape, axis)


def norm_rows(values):
    centre = jnp.mean(values, axis=-1, keepdims=True)
    shifted = values - centre
    spread = jnp.mean(shifted * shifted, axis=-1, keepdims=True)
    inverse = lax.rsqrt(spread + epsilon)
    return shifted * inverse, inverse


def norm_back(upstream, normal, inverse, scales):
    scaled = upstream * scales
    inner = (
        scaled
        - jnp.mean(scaled, axis=-1, keepdims=True)
        - normal * jnp.mean(scaled * normal, axis=-1, keepdims=True)
    )
    return inner * inverse


def pick_heads(wide, place, odd, head_size, positions):
    pair = 2 * head_size
    kept = wide[:, :pair]
    for index in range(1, positions):
        kept = jnp.where(place == index, wide[:, index * pair : (index + 1) * pair], kept)
    return jnp.where(odd, kept[:, head_size:], kept[:, :head_size])


def place_heads(out_ref, columns, places, odds, head_size, positions):
    pair = 2 * head_size
    rows = columns[0].shape[0]
    upper = iota((rows, pair), 1) >= head_size
    doubled = [
        jnp.where(upper == odd, jnp.concatenate([column, column], axis=1), 0.0)
        for column, odd in zip(columns, odds)
    ]
    for index in range(positions):
        total = jnp.zeros((rows, pair), f32)
        for value, place in zip(doubled, places):
            total = total + jnp.where(place == index, value, 0.0)
        out_ref[:, index * pair : (index + 1) * pair] = total.astype(bf16)


def lanes_of(columns, width=128):
    rows = columns[0].shape[0]
    lane = iota((rows, width), 1)
    total = jnp.zeros((rows, width), f32)
    for index, column in enumerate(columns):
        total = jnp.where(lane == index, column, total)
    return total


def soft_columns(logits):
    peak = functools.reduce(jnp.maximum, logits)
    raised = [jnp.exp(value - peak) for value in logits]
    whole = functools.reduce(lambda a, b: a + b, raised)
    return [value / whole for value in raised]


def attend_forward(
    block_rows, tokens, head_routes, expert_routes, vectors, query_weight, key_weight, value_weight,
    output_weight, head_router, expert_router,
    attn_in_out, query_out, key_out, value_out, heads_out, spread_out, hidden_out, ffn_out, columns_out,
    slots_out, wide,
):
    rows, width = tokens.shape
    head_size = key_weight.shape[1]
    positions = query_weight.shape[1] // (2 * head_size)
    top = head_routes.shape[1]
    experts = expert_router.shape[1]
    inputs = tokens[...].astype(f32)
    normal, _ = norm_rows(inputs)
    attn_in = (normal * vectors[0:1, :] + vectors[1:2, :]).astype(bf16)
    attn_in_out[...] = attn_in
    wide[...] = dot_nn(attn_in, query_weight[...])
    keys = dot_nn(attn_in, key_weight[...]).astype(bf16)
    key_out[...] = keys
    values = dot_nn(attn_in, value_weight[...]).astype(bf16)
    value_out[...] = values
    head_logits = dot_nn(attn_in, head_router[...])
    chosen = [head_routes[:, a : a + 1] for a in range(top)]
    places = [value // 2 for value in chosen]
    odds = [value % 2 == 1 for value in chosen]
    head_lane = iota(head_logits.shape, 1)
    gates = soft_columns(
        [
            jnp.sum(jnp.where(head_lane == value, head_logits, 0.0), axis=1, keepdims=True)
            for value in chosen
        ]
    )
    for a in range(top):
        picked = pick_heads(wide, places[a], odds[a], head_size, positions)
        query_out[a] = (picked.astype(bf16).astype(f32) * head_size ** (-0.5)).astype(bf16)
    totals = [[] for _ in range(top)]
    for start in range(0, rows, block_rows):
        stop = start + block_rows
        query = jnp.concatenate([query_out[a, start:stop, :] for a in range(top)], axis=0)
        scores = dot_nt(query, key_out[0:stop, :])
        row_pos = iota((top * block_rows, block_rows), 0) % block_rows
        corner = jnp.where(
            iota((top * block_rows, block_rows), 1) <= row_pos, scores[:, start:], f32(-1e30)
        )
        if start:
            scores = jnp.concatenate([scores[:, :start], corner], axis=1)
        else:
            scores = corner
        peak = jnp.max(scores, axis=1, keepdims=True)
        raised = jnp.exp(scores - peak)
        whole = jnp.sum(raised, axis=1, keepdims=True)
        output = dot_nn(raised.astype(bf16), value_out[0:stop, :]) / whole
        log_total = peak + jnp.log(whole)
        for a in range(top):
            heads_out[a, start:stop, :] = output[a * block_rows : (a + 1) * block_rows]
            totals[a].append(log_total[a * block_rows : (a + 1) * block_rows])
    totals = [jnp.concatenate(value, axis=0) for value in totals]
    columns_out[...] = lanes_of(gates + totals)
    weighted = [
        (gates[a] * heads_out[a]).astype(bf16).astype(f32) for a in range(top)
    ]
    place_heads(spread_out, weighted, places, odds, head_size, positions)
    hidden_one = inputs + dot_nn(spread_out[...], output_weight[...])
    hidden_out[...] = hidden_one
    normal_two, _ = norm_rows(hidden_one)
    ffn_in = (normal_two * vectors[2:3, :] + vectors[3:4, :]).astype(bf16)
    ffn_out[...] = ffn_in
    expert_logits = dot_nn(ffn_in, expert_router[...])
    expert_lane = iota(expert_logits.shape, 1)
    named = [expert_routes[:, c : c + 1] for c in range(2)]
    expert_gates = soft_columns(
        [
            jnp.sum(jnp.where(expert_lane == value, expert_logits, 0.0), axis=1, keepdims=True)
            for value in named
        ]
    )
    lane = iota((rows, 128), 1)
    expert = jnp.where(lane < 2 * experts, (lane // 8) * 4 + lane % 4, -1)
    first, second = expert == named[0], expert == named[1]
    hot = jnp.where(first | second, 1.0, 0.0)
    earlier = (iota((rows, rows), 1) < iota((rows, rows), 0)).astype(f32).astype(bf16)
    before = dot_nn(earlier, hot.astype(bf16))
    slot = jnp.where(hot > 0.5, before, -1.0)
    gate = jnp.where(first, expert_gates[0], jnp.where(second, expert_gates[1], 0.0))
    turned = jnp.where(lane % 8 < 4, slot, gate).T
    slots_out[...] = turned[: 2 * experts].reshape(experts // 4, 8, rows)


def attend_backward(
    block_rows, tokens, head_routes, halting, vectors, query_weight, key_weight, value_weight, output_weight,
    head_router, expert_router, attn_in, query, keys, values, heads_out, spread_out, hidden_one, ffn_in,
    columns, grad_rows, grad_logits_t, grad_hidden, state_cotan,
    tokens_grad, query_sum, output_sum, small_sum, router_two, vector_sum, wide, narrow,
):
    rows, width = tokens.shape
    head_size = key_weight.shape[1]
    heads = head_router.shape[1]
    positions = query_weight.shape[1] // (2 * head_size)
    top = head_routes.shape[1]
    gain_one, gain_two = vectors[0:1, :], vectors[2:3, :]
    normal_two, inverse_two = norm_rows(hidden_one[...])
    logits_low = grad_logits_t[...].astype(bf16)
    grad_ffn = grad_rows[...] + lax.dot_general(
        logits_low, expert_router[...], (((0,), (1,)), ((), ())), preferred_element_type=f32
    )
    router_two[...] = dot_nn(logits_low, ffn_in[...])
    gain_two_sum = jnp.sum(grad_ffn * normal_two, axis=0, keepdims=True)
    bias_two_sum = jnp.sum(grad_ffn, axis=0, keepdims=True)
    grad_one = grad_hidden[...] + norm_back(grad_ffn, normal_two, inverse_two, gain_two)
    tokens_grad[...] = grad_one
    grad_attn = grad_one.astype(bf16)
    output_sum[...] = dot_tn(spread_out[...], grad_attn)
    wide[...] = dot_nt(grad_attn, output_weight[...])
    chosen = [head_routes[:, a : a + 1] for a in range(top)]
    places = [value // 2 for value in chosen]
    odds = [value % 2 == 1 for value in chosen]
    gates = [columns[:, a : a + 1] for a in range(top)]
    grad_gates, grad_heads = [], []
    for a in range(top):
        picked = pick_heads(wide, places[a], odds[a], head_size, positions)
        grad_gates.append(jnp.sum(picked * heads_out[a], axis=1, keepdims=True))
        grad_heads.append((gates[a] * picked).astype(bf16))
    inner = functools.reduce(lambda a, b: a + b, [g * d for g, d in zip(gates, grad_gates)])
    grad_logit = [g * (d - inner) for g, d in zip(gates, grad_gates)]
    head_lane = iota((rows, heads), 1)
    grad_hot = functools.reduce(
        lambda a, b: a + b,
        [jnp.where(head_lane == chosen[a], grad_logit[a], 0.0) for a in range(top)],
    )
    grad_keys = [jnp.zeros((block_rows, head_size), f32) for _ in range(rows // block_rows)]
    grad_values = [jnp.zeros((block_rows, head_size), f32) for _ in range(rows // block_rows)]
    grad_query = [[] for _ in range(top)]
    for start in range(0, rows, block_rows):
        stop = start + block_rows
        part = slice(start, stop)
        queries = jnp.concatenate([query[a, part, :] for a in range(top)], axis=0)
        grads = jnp.concatenate([value[part] for value in grad_heads], axis=0)
        total = jnp.concatenate([columns[part, top + a : top + a + 1] for a in range(top)], axis=0)
        scores = dot_nt(queries, keys[0:stop, :])
        row_pos = iota((top * block_rows, block_rows), 0) % block_rows
        corner = jnp.where(
            iota((top * block_rows, block_rows), 1) <= row_pos, scores[:, start:], f32(-1e30)
        )
        if start:
            scores = jnp.concatenate([scores[:, :start], corner], axis=1)
        else:
            scores = corner
        prob = jnp.exp(scores - total)
        grad_prob = dot_nt(grads, values[0:stop, :])
        row_inner = jnp.sum(prob * grad_prob, axis=1, keepdims=True)
        grad_scores = (prob * (grad_prob - row_inner)).astype(bf16)
        grad_q = (dot_nn(grad_scores, keys[0:stop, :]) * head_size ** (-0.5)).astype(bf16)
        for a in range(top):
            grad_query[a].append(grad_q[a * block_rows : (a + 1) * block_rows].astype(f32))
        step_v = dot_tn(prob.astype(bf16), grads)
        step_k = dot_tn(grad_scores, queries)
        for index in range(stop // block_rows):
            piece = slice(index * block_rows, (index + 1) * block_rows)
            grad_values[index] = grad_values[index] + step_v[piece]
            grad_keys[index] = grad_keys[index] + step_k[piece]
    grad_query = [jnp.concatenate(value, axis=0) for value in grad_query]
    place_heads(narrow, grad_query, places, odds, head_size, positions)
    grad_k = jnp.concatenate(grad_keys, axis=0).astype(bf16)
    grad_v = jnp.concatenate(grad_values, axis=0).astype(bf16)
    hot_low = grad_hot.astype(bf16)
    query_sum[...] = dot_tn(attn_in[...], narrow[...])
    small_sum[:, 0:head_size] = dot_tn(attn_in[...], grad_k)
    small_sum[:, head_size : 2 * head_size] = dot_tn(attn_in[...], grad_v)
    small_sum[:, 2 * head_size : 2 * head_size + heads] = dot_tn(attn_in[...], hot_low)
    grad_in = (
        dot_nt(narrow[...], query_weight[...])
        + dot_nt(grad_k, key_weight[...])
        + dot_nt(grad_v, value_weight[...])
        + dot_nt(hot_low, head_router[...])
    )
    normal_one, inverse_one = norm_rows(tokens[...].astype(f32))
    vector_sum[0:1, :] = jnp.sum(grad_in * normal_one, axis=0, keepdims=True)
    vector_sum[1:2, :] = jnp.sum(grad_in, axis=0, keepdims=True)
    vector_sum[2:3, :] = gain_two_sum
    vector_sum[3:4, :] = bias_two_sum
    vector_sum[4:8, :] = jnp.zeros((4, width), f32)
    tokens_grad[...] = (
        tokens_grad[...]
        + norm_back(grad_in, normal_one, inverse_one, gain_one)
        + (1.0 - halting[...].astype(f32)) * state_cotan[...].astype(f32)
    )


def expert_exchange(
    capacity, chunks,
    ffn_in, slots, tokens, hidden_one, state_cotan, accum_cotan, scalars, vectors, first_hbm, second_hbm,
    new_state, accum_part, columns_out, grad_hidden, grad_rows, grad_logits_t, halt_sum, in_terms, out_terms,
    first, second, column, gathered, grads_in, cross, act, slope, produced, crossed, grad_out, grad_crossed,
    partial, landed, staged, keys, shares, share_out,
    weight_sem, key_send, key_recv, gather_send, gather_recv, cross_send, cross_recv, back_send, back_recv,
    reduce_send, reduce_recv, share_send, share_recv, stage_sem,
):
    rows, width = ffn_in.shape
    local, _, hidden_size = first.shape
    tile = width
    tiles = hidden_size // tile
    piece = rows // chunks
    me = lax.axis_index("expert")
    z, x = me // 2, me % 2
    other = 1 - x
    low = z < 2
    middle = (z == 1) | (z == 2)
    edge = jnp.logical_not(middle)

    def real(mirrored):
        return jnp.where(low, mirrored, 3 - mirrored)

    def along(depth):
        return {"expert": depth * 2 + x}

    across = {"expert": z * 2 + other}

    def order(j):
        return real(jnp.where(middle, jnp.where(j < 2, 1 - j, j), j))

    barrier = pltpu.get_barrier_semaphore()
    for step in range(1, 4):
        pl.semaphore_signal(barrier, inc=1, device_id=along((z + step) % 4), device_id_type=MESH)
    pl.semaphore_signal(barrier, inc=1, device_id=across, device_id_type=MESH)
    loads = [
        pltpu.make_async_copy(first_hbm, first, weight_sem.at[0]),
        pltpu.make_async_copy(second_hbm, second, weight_sem.at[1]),
    ]
    for load in loads:
        load.start()
    column[0, z] = ffn_in[...]
    keys[z] = slots[z]
    pl.semaphore_wait(barrier, 4)

    def key_copy(step):
        there = (z + step) % 4
        return pltpu.make_async_remote_copy(
            src_ref=slots.at[there], dst_ref=keys.at[z], send_sem=key_send.at[step], recv_sem=key_recv.at[z],
            device_id=along(there), device_id_type=MESH,
        )

    def key_arrival(shard):
        return pltpu.make_async_remote_copy(
            src_ref=slots.at[0], dst_ref=keys.at[shard], send_sem=key_send.at[0], recv_sem=key_recv.at[shard],
            device_id=across, device_id_type=MESH,
        )

    def gather_copy(phase, source, shard, depth, index):
        return pltpu.make_async_remote_copy(
            src_ref=source, dst_ref=column.at[phase, shard], send_sem=gather_send.at[phase, index],
            recv_sem=gather_recv.at[phase, shard], device_id=along(depth), device_id_type=MESH,
        )

    def send_own(phase, source):
        @pl.when(edge)
        def _():
            gather_copy(phase, source, z, real(1), 0).start()

        @pl.when(middle)
        def _():
            gather_copy(phase, source, z, real(0), 0).start()
            gather_copy(phase, source, z, real(2), 1).start()

    def forward(phase, mirrored, target, index):
        shard = real(mirrored)
        return gather_copy(phase, column.at[phase, shard], shard, real(target), index)

    def finish_gather(phase, source):
        gather_copy(phase, source, z, real(1), 0).wait_send()

        @pl.when(middle)
        def _():
            gather_copy(phase, source, z, real(2), 1).wait_send()
            forward(phase, 0, 2, 2).wait_send()
            forward(phase, 2, 0, 3).wait_send()
            forward(phase, 3, 0, 4).wait_send()

    def await_shard(phase, mirrored):
        shard = real(mirrored)
        if phase == 0:
            key_arrival(shard).wait_recv()
        gather_copy(phase, column.at[phase, shard], shard, z, 0).wait_recv()

    def await_shards(phase, j):
        @pl.when(edge & (j > 0))
        def _():
            await_shard(phase, j)

        @pl.when(middle & (j == 1))
        def _():
            await_shard(phase, 0)
            forward(phase, 0, 2, 2).start()
            await_shard(phase, 2)
            forward(phase, 2, 0, 3).start()

        @pl.when(middle & (j == 2))
        def _():
            await_shard(phase, 3)
            forward(phase, 3, 0, 4).start()

    def experts_of(shard):
        table = keys[shard]
        found = []
        for own in (True, False):
            for r in range(local):
                here, there = (r, local + r) if own else (local + r, r)
                line = jnp.where(x == 0, table[here : here + 1], table[there : there + 1])
                gate = jnp.where(x == 0, table[4 + here : 5 + here], table[4 + there : 5 + there])
                mask = iota((capacity, rows), 0).astype(f32) == line
                found.append((mask, jnp.sum(jnp.where(mask, gate, 0.0), axis=1, keepdims=True)))
        return found

    def hot_rows(found):
        return jnp.concatenate([jnp.where(mask, 1.0, 0.0).astype(bf16) for mask, _ in found], axis=0)

    def cross_copy(phase, shard, r):
        target = gathered if phase == 0 else grads_in
        return pltpu.make_async_remote_copy(
            src_ref=cross.at[shard, r], dst_ref=target.at[4 + shard, r], send_sem=cross_send.at[phase, shard, r],
            recv_sem=cross_recv.at[phase, shard, r], device_id=across, device_id_type=MESH,
        )

    def back_copy(phase, shard, r):
        source, target = (produced, crossed) if phase == 0 else (grad_out, grad_crossed)
        return pltpu.make_async_remote_copy(
            src_ref=source.at[4 + shard, r], dst_ref=target.at[shard, r], send_sem=back_send.at[phase, shard, r],
            recv_sem=back_recv.at[phase, shard, r], device_id=across, device_id_type=MESH,
        )

    def share_copy(shard):
        return pltpu.make_async_remote_copy(
            src_ref=share_out.at[shard], dst_ref=shares.at[z], send_sem=share_send.at[shard],
            recv_sem=share_recv.at[z], device_id=along(shard), device_id_type=MESH,
        )

    def dispatch(phase, shard):
        found = experts_of(shard)
        taken = dot_nn(hot_rows(found), column[phase, shard])
        lines = []
        for index, (mask, gate) in enumerate(found):
            part = taken[index * capacity : (index + 1) * capacity]
            if phase == 1:
                part = gate * part
            r = index % local
            if index < local:
                (gathered if phase == 0 else grads_in)[shard, r] = part.astype(bf16)
            else:
                cross[shard, r] = part.astype(bf16)
                cross_copy(phase, shard, r).start()
            if phase == 1:
                value = (produced if index < local else crossed)[shard, r].astype(f32)
                inner = jnp.sum(part * value, axis=1, keepdims=True)
                lines.append(jnp.sum(jnp.where(mask, inner, 0.0), axis=0, keepdims=True))
        if phase == 1:
            own, far = lines[:local], lines[local:]
            stack = [jnp.where(x == 0, a, b) for a, b in zip(own + far, far + own)]
            share_out[shard] = jnp.concatenate(stack + [jnp.zeros((4, rows), f32)], axis=0)

            @pl.when(shard == z)
            def _():
                shares[z] = share_out[z]

            @pl.when(shard != z)
            def _():
                share_copy(shard).start()

    def expert_forward(shard):
        def one(r, carry):
            cross_copy(0, shard, r).wait_recv()
            taken = jnp.concatenate([gathered[shard, r], gathered[4 + shard, r]], axis=0)
            total = jnp.zeros((2 * capacity, width), f32)
            for n in range(tiles):
                part = slice(n * tile, (n + 1) * tile)
                pre = dot_nn(taken, first[r, :, part])
                cumulative = 0.5 * (1.0 + lax.erf(pre * (1.0 / math.sqrt(2.0))))
                density = jnp.exp(-0.5 * pre * pre) * (1.0 / math.sqrt(2.0 * math.pi))
                inner = (pre * cumulative).astype(bf16)
                steep = (cumulative + pre * density).astype(bf16)
                act[shard, r, :, part] = inner[:capacity]
                act[4 + shard, r, :, part] = inner[capacity:]
                slope[shard, r, :, part] = steep[:capacity]
                slope[4 + shard, r, :, part] = steep[capacity:]
                total = total + dot_nn(inner, second[r, part, :])
            produced[shard, r] = total[:capacity].astype(bf16)
            produced[4 + shard, r] = total[capacity:].astype(bf16)
            back_copy(0, shard, r).start()
            return carry

        lax.fori_loop(0, local, one, 0)

    def expert_backward(shard):
        def one(r, carry):
            cross_copy(1, shard, r).wait_recv()
            taken = jnp.concatenate([grads_in[shard, r], grads_in[4 + shard, r]], axis=0)
            total = jnp.zeros((2 * capacity, width), f32)
            for n in range(tiles):
                part = slice(n * tile, (n + 1) * tile)
                grad = dot_nt(taken, second[r, part, :])
                steep = jnp.concatenate([slope[shard, r, :, part], slope[4 + shard, r, :, part]], axis=0)
                grad_pre = (grad * steep.astype(f32)).astype(bf16)
                slope[shard, r, :, part] = grad_pre[:capacity]
                slope[4 + shard, r, :, part] = grad_pre[capacity:]
                total = total + dot_nt(grad_pre, first[r, :, part])
            grad_out[shard, r] = total[:capacity].astype(bf16)
            grad_out[4 + shard, r] = total[capacity:].astype(bf16)
            back_copy(1, shard, r).start()
            return carry

        lax.fori_loop(0, local, one, 0)

    def reduce_copy(phase, shard, index, chunk, depth):
        part = pl.ds(pl.multiple_of(chunk * piece, piece), piece)
        return pltpu.make_async_remote_copy(
            src_ref=partial.at[shard, part], dst_ref=landed.at[phase, index, part],
            send_sem=reduce_send.at[phase, index, chunk], recv_sem=reduce_recv.at[phase, index, chunk],
            device_id=along(depth), device_id_type=MESH,
        )

    def combine(phase, j):
        shard = order(j)
        for r in range(local):
            back_copy(phase, shard, r).wait_recv()
        found = experts_of(shard)
        if phase == 0:
            pieces = [
                gate * (produced if index < local else crossed)[shard, index % local].astype(f32)
                for index, (_, gate) in enumerate(found)
            ]
            pieces = [value.astype(bf16) for value in pieces]
        else:
            pieces = [
                (grad_out if index < local else grad_crossed)[shard, index % local]
                for index in range(2 * local)
            ]
        partial[shard] = dot_tn(hot_rows(found), jnp.concatenate(pieces, axis=0)).astype(bf16)

        @pl.when(edge & (j > 0))
        def _():
            for chunk in range(chunks):
                reduce_copy(phase, shard, j - 1, chunk, real(1)).start()

    def pass_on(phase, chunk, source, mirrored, index, depth):
        shard = real(mirrored)
        reduce_copy(phase, shard, source, chunk, z).wait_recv()
        part = pl.ds(pl.multiple_of(chunk * piece, piece), piece)
        partial[shard, part] = (
            partial[shard, part].astype(f32) + landed[phase, source, part].astype(f32)
        ).astype(bf16)
        reduce_copy(phase, shard, index, chunk, depth).start()

    def reduce_rows(phase, filler):
        def step(i, carry):
            @pl.when(middle & (i < chunks))
            def _():
                pass_on(phase, i, 1, 2, 3, real(2))

            @pl.when(middle & (i >= chunks))
            def _():
                pass_on(phase, i - chunks, 2, 3, 4, real(2))
                pass_on(phase, i - chunks, 4, 0, 0, real(0))

            filler(i)
            return carry

        lax.fori_loop(0, 2 * chunks, step, 0)

    def reduced(phase):
        for chunk in range(chunks):
            reduce_copy(phase, z, 0, chunk, z).wait_recv()
        total = partial[z].astype(f32) + landed[phase, 0].astype(f32)

        @pl.when(middle)
        def _():
            for chunk in range(chunks):
                reduce_copy(phase, z, 3, chunk, z).wait_recv()

        return total + jnp.where(middle, landed[phase, 3].astype(f32), 0.0)

    def finish_reduce(phase):
        @pl.when(edge)
        def _():
            for index in range(3):
                for chunk in range(chunks):
                    reduce_copy(phase, real(index + 1), index, chunk, real(1)).wait_send()

        @pl.when(middle)
        def _():
            for chunk in range(chunks):
                reduce_copy(phase, real(2), 3, chunk, real(2)).wait_send()
                reduce_copy(phase, real(3), 4, chunk, real(2)).wait_send()
                reduce_copy(phase, real(0), 0, chunk, real(0)).wait_send()

    def finish_cross(phase):
        for shard in range(4):
            for r in range(local):
                cross_copy(phase, shard, r).wait_send()
                back_copy(phase, shard, r).wait_send()

    def run(phase, experts):
        def step(j, carry):
            @pl.when(j >= 2)
            def _():
                combine(phase, j - 2)

            @pl.when((j >= 1) & (j <= 4))
            def _():
                experts(order(j - 1))

            @pl.when(j <= 3)
            def _():
                await_shards(phase, j)
                dispatch(phase, order(j))

            return carry

        lax.fori_loop(0, 6, step, 0)

    for step in range(1, 4):
        key_copy(step).start()
    send_own(0, ffn_in)
    for load in loads:
        load.wait()
    run(0, expert_forward)
    reduce_rows(0, lambda i: None)
    hidden = hidden_one[...] + reduced(0)
    remain, active, remain_cotan = scalars[:, 0:1], scalars[:, 1:2], scalars[:, 2:3]
    halt_vector = vectors[4:5, :]
    halt_prob = jax.nn.sigmoid(jnp.sum(hidden * halt_vector, axis=1, keepdims=True))
    halt_share = active * remain * halt_prob
    grad_accum = accum_cotan[...].astype(f32)
    grad_share = jnp.sum(grad_accum * hidden, axis=1, keepdims=True)
    grad_logit = active * remain * (grad_share - remain_cotan) * halt_prob * (1.0 - halt_prob)
    grad_here = active * state_cotan[...].astype(f32) + halt_share * grad_accum + grad_logit * halt_vector
    grad_hidden[...] = grad_here
    column[1, z] = grad_here.astype(bf16)
    send_own(1, column.at[1, z])
    new_state[...] = jnp.where(active > 0.5, hidden, tokens[...].astype(f32)).astype(bf16)
    accum_part[...] = halt_share * hidden
    columns_out[...] = lanes_of(
        [
            remain * (1.0 - active * halt_prob),
            active * halt_prob * grad_share + (1.0 - active * halt_prob) * remain_cotan,
        ]
    )
    halt_sum[...] = jnp.concatenate(
        [jnp.sum(grad_logit * hidden, axis=0, keepdims=True), jnp.zeros((7, width), f32)], axis=0
    )
    for step in range(1, 4):
        key_copy(step).wait_send()
    finish_gather(0, ffn_in)
    finish_cross(0)
    finish_reduce(0)
    run(1, expert_backward)

    def stage_in(r, n, slot):
        part = pl.ds(pl.multiple_of(n * tile, tile), tile)
        return pltpu.make_async_copy(staged.at[slot], in_terms.at[r, :, part], stage_sem.at[slot])

    def stage_out(r, n, slot):
        part = pl.ds(pl.multiple_of(n * tile, tile), tile)
        return pltpu.make_async_copy(staged.at[slot], out_terms.at[r, part, :], stage_sem.at[slot])

    def weight_terms(i):
        r, n = i // tiles, i % tiles
        part = pl.ds(pl.multiple_of(n * tile, tile), tile)
        total = local * 4 * capacity

        @pl.when(i > 0)
        def _():
            stage_in(0, 0, 0).wait()
            stage_out(0, 0, 1).wait()

        left = gathered[:, r].reshape(total, width)
        right = slope[:, r, :, part].reshape(total, tile)
        staged[0] = dot_tn(left, right).astype(bf16)
        stage_in(r, n, 0).start()
        left = act[:, r, :, part].reshape(total, tile)
        right = grads_in[:, r].reshape(total, width)
        staged[1] = dot_tn(left, right).astype(bf16)
        stage_out(r, n, 1).start()

    reduce_rows(1, weight_terms)
    stage_in(0, 0, 0).wait()
    stage_out(0, 0, 1).wait()
    for step in range(1, 4):
        shard = (z + step) % 4
        pltpu.make_async_remote_copy(
            src_ref=share_out.at[0], dst_ref=shares.at[shard], send_sem=share_send.at[0],
            recv_sem=share_recv.at[shard], device_id=across, device_id_type=MESH,
        ).wait_recv()
        share_copy(shard).wait_send()
    share = jnp.concatenate([shares[s, 0:4] for s in range(4)], axis=0)
    gate = jnp.concatenate([slots[s, 4:8] for s in range(4)], axis=0)
    grad_logits_t[...] = share - gate * jnp.sum(share, axis=0, keepdims=True)
    grad_rows[...] = reduced(1)
    finish_gather(1, column.at[1, z])
    finish_cross(1)
    finish_reduce(1)


def slot_targets(routes, experts, room_rows):
    flattened = routes.reshape(-1)
    hot_rows = (flattened[:, None] == jnp.arange(experts, dtype=jnp.int32)[None, :]).astype(jnp.int32)
    before = jnp.cumsum(hot_rows, axis=0) - hot_rows
    return flattened * room_rows + jnp.sum(hot_rows * before, axis=1)


def experts_by_all_to_all(
    capacity, tokens, remain, halting, expert_routes, halt_weight, expert_router, expert_in, expert_out,
    state_cotan, accum_cotan, remain_cotan, hidden_one, ffn_in,
):
    rows, width = tokens.shape
    experts = expert_router.shape[1]
    top = expert_routes.shape[1]
    highest = lax.Precision.HIGHEST
    inputs = tokens.astype(f32)
    active = halting.astype(f32)
    expert_logits = jnp.dot(ffn_in, expert_router, preferred_element_type=f32)
    expert_gate = jax.nn.softmax(jnp.take_along_axis(expert_logits, expert_routes, axis=1), axis=1)
    targets = slot_targets(expert_routes, experts, capacity)

    def spread(values):
        placed = jnp.zeros((experts * capacity, width), bf16).at[targets].set(values)
        return lax.all_to_all(
            placed.reshape(experts, capacity, width), "expert", split_axis=0, concat_axis=1, tiled=True
        )

    def collect(values):
        back = lax.all_to_all(values, "expert", split_axis=1, concat_axis=0, tiled=True)
        back = back.reshape(experts * capacity, width)
        return back[targets].astype(f32).reshape(rows, top, width)

    arrived = spread(jnp.repeat(ffn_in, top, axis=0))
    pre_act = jnp.einsum("erd,edf->erf", arrived, expert_in, preferred_element_type=f32)
    inner_act = jax.nn.gelu(pre_act, approximate=False).astype(bf16)
    produced = jnp.einsum("erf,efd->erd", inner_act, expert_out, preferred_element_type=f32).astype(bf16)
    picked = collect(produced)
    hidden = hidden_one + jnp.sum(expert_gate[:, :, None] * picked, axis=1)
    halt_vector = halt_weight.astype(f32)
    halt_prob = jax.nn.sigmoid(jnp.dot(hidden, halt_vector, precision=highest))
    halt_share = active * remain * halt_prob
    new_state = jnp.where(active[:, None] > 0.5, hidden, inputs).astype(bf16)
    accum_part = halt_share[:, None] * hidden
    remain_left = remain * (1.0 - active * halt_prob)
    grad_accum = accum_cotan.astype(f32)
    grad_share = jnp.sum(grad_accum * hidden, axis=1)
    grad_logit = active * remain * (grad_share - remain_cotan) * halt_prob * (1.0 - halt_prob)
    remain_grad = active * halt_prob * grad_share + (1.0 - active * halt_prob) * remain_cotan
    grad_hidden = (
        active[:, None] * state_cotan.astype(f32)
        + halt_share[:, None] * grad_accum
        + grad_logit[:, None] * halt_vector[None, :]
    )
    halt_sum = jnp.dot(grad_logit, hidden, precision=highest)
    grad_gate = jnp.sum(grad_hidden[:, None, :] * picked, axis=2)
    grad_chosen = expert_gate * (grad_gate - jnp.sum(expert_gate * grad_gate, axis=1, keepdims=True))
    expert_hot = (expert_routes[:, :, None] == jnp.arange(experts, dtype=jnp.int32)[None, None, :]).astype(f32)
    grad_logits = jnp.einsum("tk,tke->te", grad_chosen, expert_hot, precision=highest)
    grad_prod = (expert_gate[:, :, None] * grad_hidden[:, None, :]).astype(bf16)
    grad_arrived = spread(grad_prod.reshape(rows * top, width))
    grad_inner = jnp.einsum("erd,efd->erf", grad_arrived, expert_out, preferred_element_type=f32)
    cumulative = 0.5 * (1.0 + lax.erf(pre_act * (1.0 / math.sqrt(2.0))))
    density = jnp.exp(-0.5 * pre_act * pre_act) * (1.0 / math.sqrt(2.0 * math.pi))
    grad_pre = (grad_inner * (cumulative + pre_act * density)).astype(bf16)
    grad_rows = jnp.einsum("erf,edf->erd", grad_pre, expert_in, preferred_element_type=f32).astype(bf16)
    in_terms = jnp.einsum("erd,erf->edf", arrived, grad_pre, preferred_element_type=f32)
    out_terms = jnp.einsum("erf,erd->efd", inner_act, grad_arrived, preferred_element_type=f32)
    return (
        new_state, accum_part, remain_left, remain_grad, grad_hidden, jnp.sum(collect(grad_rows), axis=1),
        grad_logits.T, halt_sum, in_terms.astype(bf16), out_terms.astype(bf16),
    )


def vmem(count):
    return [pl.BlockSpec(memory_space=pltpu.VMEM)] * count


def hbm(count):
    return [pl.BlockSpec(memory_space=pl.ANY)] * count


def experts_on_lines(
    capacity, chunks, tokens, scalars, vectors, expert_in, expert_out, state_cotan, accum_cotan, hidden_one, ffn_in,
    slots,
):
    rows, width = tokens.shape
    local, _, hidden_size = expert_in.shape
    shape, buffer, flags = jax.ShapeDtypeStruct, pltpu.VMEM, pltpu.SemaphoreType.DMA
    results = pl.pallas_call(
        functools.partial(expert_exchange, capacity, chunks),
        out_shape=[
            shape((rows, width), bf16),
            shape((rows, width), f32),
            shape((rows, 128), f32),
            shape((rows, width), f32),
            shape((rows, width), f32),
            shape((8 * local, rows), f32),
            shape((8, width), f32),
            shape((local, width, hidden_size), bf16),
            shape((local, hidden_size, width), bf16),
        ],
        in_specs=vmem(8) + hbm(2),
        out_specs=vmem(7) + hbm(2),
        scratch_shapes=[
            buffer((local, width, hidden_size), bf16),
            buffer((local, hidden_size, width), bf16),
            buffer((2, 4, rows, width), bf16),
            buffer((8, local, capacity, width), bf16),
            buffer((8, local, capacity, width), bf16),
            buffer((4, local, capacity, width), bf16),
            buffer((8, local, capacity, hidden_size), bf16),
            buffer((8, local, capacity, hidden_size), bf16),
            buffer((8, local, capacity, width), bf16),
            buffer((4, local, capacity, width), bf16),
            buffer((8, local, capacity, width), bf16),
            buffer((4, local, capacity, width), bf16),
            buffer((4, rows, width), bf16),
            buffer((2, 5, rows, width), bf16),
            buffer((2, width, width), bf16),
            buffer((4, 8, rows), f32),
            buffer((4, 8, rows), f32),
            buffer((4, 8, rows), f32),
            flags((2,)),
            flags((4,)),
            flags((4,)),
            flags((2, 5)),
            flags((2, 4)),
            flags((2, 4, local)),
            flags((2, 4, local)),
            flags((2, 4, local)),
            flags((2, 4, local)),
            flags((2, 5, chunks)),
            flags((2, 5, chunks)),
            flags((4,)),
            flags((4,)),
            flags((2,)),
        ],
        compiler_params=pltpu.CompilerParams(
            vmem_limit_bytes=VMEM_LIMIT, collective_id=1, has_side_effects=True
        ),
        name="expert_exchange",
    )(ffn_in, slots, tokens, hidden_one, state_cotan, accum_cotan, scalars, vectors, expert_in, expert_out)
    new_state, accum_part, pair, grad_hidden, grad_rows, grad_logits_t, halt_sum, in_terms, out_terms = results
    return (
        new_state, accum_part, pair[:, 0], pair[:, 1], grad_hidden, grad_rows, grad_logits_t, halt_sum[0], in_terms,
        out_terms,
    )


def body(
    mesh_sizes, tokens, remain, halting, head_routes, expert_routes, first_gain, first_bias, query_weight,
    key_weight, value_weight, output_weight, head_router, second_gain, second_bias, expert_router, expert_in,
    expert_out, halt_weight, state_cotan, accum_cotan, remain_cotan,
):
    rows, width = tokens.shape
    head_size = key_weight.shape[1]
    top = head_routes.shape[1]
    wide_size = query_weight.shape[1]
    experts = expert_router.shape[1]
    heads = head_router.shape[1]
    capacity = 4 * rows // experts
    shape = jax.ShapeDtypeStruct
    vectors = jnp.stack(
        [first_gain, first_bias, second_gain, second_bias, halt_weight, halt_weight, halt_weight, halt_weight]
    ).astype(f32)
    scalars = jnp.stack([remain, halting.astype(f32), remain_cotan], axis=1)
    attn_in, query, keys, values, heads_out, spread_out, hidden_one, ffn_in, columns, slots = pl.pallas_call(
        functools.partial(attend_forward, 128),
        out_shape=[
            shape((rows, width), bf16),
            shape((top, rows, head_size), bf16),
            shape((rows, head_size), bf16),
            shape((rows, head_size), bf16),
            shape((top, rows, head_size), f32),
            shape((rows, wide_size), bf16),
            shape((rows, width), f32),
            shape((rows, width), bf16),
            shape((rows, 128), f32),
            shape((experts // 4, 8, rows), f32),
        ],
        in_specs=vmem(10),
        out_specs=vmem(10),
        scratch_shapes=[pltpu.VMEM((rows, wide_size), f32)],
        compiler_params=pltpu.CompilerParams(vmem_limit_bytes=VMEM_LIMIT),
        name="attend_forward",
    )(
        tokens, head_routes, expert_routes, vectors, query_weight, key_weight, value_weight, output_weight,
        head_router, expert_router,
    )
    if mesh_sizes == (4, 8):
        stage = experts_on_lines(
            capacity, 4, tokens, scalars, vectors, expert_in, expert_out, state_cotan, accum_cotan, hidden_one,
            ffn_in, slots,
        )
    else:
        stage = experts_by_all_to_all(
            capacity, tokens, remain, halting, expert_routes, halt_weight, expert_router, expert_in, expert_out,
            state_cotan, accum_cotan, remain_cotan, hidden_one, ffn_in,
        )
    (new_state, accum_part, remain_left, remain_grad, grad_hidden, grad_rows, grad_logits_t, halt_sum, in_terms,
     out_terms) = stage
    expert_in_grad = lax.psum_scatter(in_terms, "dp", scatter_dimension=2, tiled=True).astype(f32)
    expert_out_grad = lax.psum_scatter(out_terms, "dp", scatter_dimension=1, tiled=True).astype(f32)
    tokens_grad, query_sum, output_sum, small_sum, router_two, vector_sum = pl.pallas_call(
        functools.partial(attend_backward, 128),
        out_shape=[
            shape((rows, width), f32),
            shape((width, wide_size), f32),
            shape((wide_size, width), f32),
            shape((width, 256), f32),
            shape((experts, width), f32),
            shape((8, width), f32),
        ],
        in_specs=vmem(23),
        out_specs=vmem(6),
        scratch_shapes=[pltpu.VMEM((rows, wide_size), f32), pltpu.VMEM((rows, wide_size), bf16)],
        compiler_params=pltpu.CompilerParams(vmem_limit_bytes=VMEM_LIMIT),
        name="attend_backward",
    )(
        tokens, head_routes, halting[:, None], vectors, query_weight, key_weight, value_weight, output_weight,
        head_router, expert_router, attn_in, query, keys, values, heads_out, spread_out, hidden_one, ffn_in,
        columns, grad_rows, grad_logits_t, grad_hidden, state_cotan,
    )
    totals = lax.psum(
        (query_sum, output_sum, small_sum, router_two, vector_sum, halt_sum), ("dp", "expert")
    )
    query_grad, output_grad, small, router, vector, halt_grad = totals
    return (
        new_state,
        accum_part,
        remain_left,
        tokens_grad,
        remain_grad,
        vector[0],
        vector[1],
        query_grad,
        small[:, :head_size],
        small[:, head_size : 2 * head_size],
        output_grad,
        small[:, 2 * head_size : 2 * head_size + heads],
        vector[2],
        vector[3],
        router.T,
        expert_in_grad,
        expert_out_grad,
        halt_grad,
    )


def solution(mesh):
    in_specs = (
        P(("dp", "expert"), None),
        P(("dp", "expert")),
        P(("dp", "expert")),
        P(("dp", "expert"), None),
        P(("dp", "expert"), None),
        P(),
        P(),
        P(),
        P(),
        P(),
        P(),
        P(),
        P(),
        P(),
        P(),
        P("expert", None, None),
        P("expert", None, None),
        P(),
        P(("dp", "expert"), None),
        P(("dp", "expert"), None),
        P(("dp", "expert")),
    )
    out_specs = (
        P(("dp", "expert"), None),
        P(("dp", "expert"), None),
        P(("dp", "expert")),
        P(("dp", "expert"), None),
        P(("dp", "expert")),
        P(),
        P(),
        P(),
        P(),
        P(),
        P(),
        P(),
        P(),
        P(),
        P(),
        P("expert", None, "dp"),
        P("expert", "dp", None),
        P(),
    )
    sizes = (mesh.shape["dp"], mesh.shape["expert"])
    run = functools.partial(body, sizes)
    return jax.shard_map(run, mesh=mesh, in_specs=in_specs, out_specs=out_specs, check_vma=False)
```

time: 841 us -> 454 us (0.54); the launches traced: 832 us -> 453 us
  Pallas kernels: 4.69 us -> 216 us
  waiting for transfers between devices: 335 us -> 143 us
  matrix products: 129 us -> 0 us
  local copies, waits for them, and re-layouts: 142 us -> 29.2 us
  other arithmetic: 86.6 us -> 7.83 us
  blocking collectives: 108 us -> 41.7 us
  starting transfers between devices: 9.08 us -> 0.12 us
    pallas_call x0 -> x3, Pallas kernels: none -> 216 us  [the longest x1 178 us: experts_on_lines(): pl.pallas_call(functools.partial(expert_exchange, capacity, chunks), out_...]
    psum x2 -> x1, waiting for transfers between devices: 275 us -> 142 us  [body(): lax.psum((query_sum, output_sum, small_sum, router_two, vector_sum, halt_...]
    dot_general x37 -> x0, matrix products: 129 us -> none  [the longest x1 17.2 us: body(): jnp.einsum('erd,edf->erf', arrived, expert_in, preferred_element_type=jnp...]
    all_to_all x2 -> x0, blocking collectives: 108 us -> none  [the longest x1 55.7 us: body(): lax.all_to_all(outgoing.reshape(experts_all, capacity, model_width), 'exp...]
    all_to_all x2 -> x0, waiting for transfers between devices: 59.4 us -> none  [the longest x1 34.1 us: body(): lax.all_to_all(produced, 'expert', split_axis=1, concat_axis=0, tiled=True)]
    convert_element_type x14 -> x4, other arithmetic: 49.4 us -> 7.12 us  [the longest x1 2.99 us: body(): lax.psum_scatter(in_terms, 'dp', scatter_dimension=2, tiled=True)]
    psum x0 -> x1, blocking collectives: none -> 41.7 us  [body(): lax.psum((query_sum, output_sum, small_sum, router_two, vector_sum, halt_...]
    gather x12 -> x0, local copies, waits for them, and re-layouts: 40 us -> none  [the longest x5 17.5 us: body(): jnp.take_along_axis(head_logits, head_routes, axis=1)]
  transfers between devices with their start and end apart: 6 -> 3, of which waited for: 4 -> 1; matrix products, arithmetic and copies ran while one was open for 18% -> 2% of each run, Pallas kernels for 0% -> 0%
where the time goes in v1:
time: 454 us; the launch traced here: 453 us
  Pallas kernels  216 us (48%)
  waiting for transfers between devices  143 us (31%)
  blocking collectives  41.7 us (9%)
  local copies, waits for them, and re-layouts  29.2 us (6%)
  between operations  15.6 us (3%)
  other arithmetic  7.83 us (2%)
    pallas_call x1, Pallas kernels, experts_on_lines(): pl.pallas_call(functools.partial(expert_exchange, capacity, chunks), out_...  178 us
    psum x1, waiting for transfers between devices, body(): lax.psum((query_sum, output_sum, small_sum, router_two, vector_sum, halt_...  142 us
    psum x1, blocking collectives, body(): lax.psum((query_sum, output_sum, small_sum, router_two, vector_sum, halt_...  41.7 us
    pallas_call x1, Pallas kernels, body(): pl.pallas_call(functools.partial(attend_backward, 128), out_shape=[shape(...  25.2 us
    unnamed x25, local copies, waits for them, and re-layouts  19.1 us
    pallas_call x1, Pallas kernels, body(): pl.pallas_call(functools.partial(attend_forward, 128), out_shape=[shape((...  13.4 us
  transfers between devices with their start and end apart: 3, of which 1 were waited for; matrix products, arithmetic and copies ran while one was open for 2% of the time, Pallas kernels for 0%

profile of v1, /device:TPU:0, one launch (start us, length us, event | category | flops | bytes accessed | tf_op | source)
XLA Modules:
  0.0 453.5 jit_solution(5220613145880656782)
XLA Ops:
  8.1 0.7 stack.33
  8.8 0.7 stack.34
  9.4 0.7 stack.35
  11.5 0.7 convert_element_type.13
  12.8 1.6 copy.73.key_weight
  14.4 1.6 copy.74.value_weight
  16.0 1.5 copy.75.head_router
  17.5 1.5 copy.76.expert_router
  19.0 0.7 pad_maximum_fusion
  19.7 0.9 copy.77.scalars
  20.5 1.5 copy.71.head_routes
  22.1 1.5 copy.72.expert_routes
  23.6 1.5 copy.79.halting
  25.2 13.4 %attend_forward.1 = (bf16[512,512]{1,0:T(8,128)(2,1)}, bf16[4,512,64]{2,1,0:T(8,128)(2,1)}, bf16[512,64]{1,0:T(8,128)(2,1)}, bf16[512,64]{1,0:T(8,128)(2,1)}, f3...) custom-call(bf16[512,512]{1,0:T(8,128)(2,1)} %tokens.5, ...), custom_call_target="tpu_custom_call" | custom-call | tf_op jit(solution)/shard_map/attend_forward/pallas_call | solution.py:856
  38.6 177.5 %expert_exchange.1 = (bf16[512,512]{1,0:T(8,128)(2,1)}, f32[512,512]{1,0:T(8,128)}, f32[512,128]{1,0:T(8,128)}, f32[512,512]{1,0:T(8,128)}, f32[512,512]{1,0:T(8...) custom-call(bf16[512,512]{1,0:T(8,128)(2,1)} %get-tuple-element.43.f, ...), custom_call_target="tpu_custom_call" | custom-call | tf_op jit(solution)/shard_map/expert_exchange/pallas_call | solution.py:778
  216.1 25.2 %attend_backward.1 = (f32[512,512]{1,0:T(8,128)}, f32[512,1536]{1,0:T(8,128)}, f32[1536,512]{1,0:T(8,128)}, f32[512,256]{1,0:T(8,128)}, f32[16,512]{1,0:T(8,128)}, /*index=5*/f32[8,512]{1,0:T(8,128)}) custom-call(bf16[512,512]{1,0:T(8,128)(2,1)} %tokens.5, s32[512,4]{1,0:T(8,128)} %copy.71.head_routes, s32[512,1]{1,0:T(8,128)} %copy.79.halting, ...), custom_call_target="tpu_custom_call" | custom-call | tf_op jit(solution)/shard_map/attend_backward/pallas_call | solution.py:893
  242.5 0.7 slice.39
  243.2 41.7 %all-reduce = (f32[8,512]{1,0:T(8,128)S(1)}, f32[512,16]{0,1:T(8,128)}, f32[512]{0:T(512)}) all-reduce(f32[8,512]{1,0:T(8,128)S(1)} %copy-done.5, f32[512,16]{0,1:T(8,128)S(1)} %bitcast.10, f32[512]{0:T(512)S(1)} %bitcast.13), channel_id=1, replica_groups=mesh['dp'=4,'expert'=8] {'dp','expert'}, use_global_device_ids=true, to_apply=%region_0.0 | all-reduce | flops 12800 | bytes 102400 | tf_op jit(solution)/shard_map/psum | solution.py:913
  284.9 0.9 slice_reduce_fusion
  286.4 141.9 %all-reduce.4.cloned.1.call-done = (f32[512,1536]{1,0:T(8,128)}, f32[512,256]{1,0:T(8,128)}, f32[1536,512]{1,0:T(8,128)}) async-done(((f32[512,1536]{1,0:T(8,128)}, f32[512,256]{1,0:T(8,128)}, f32[1536,512]{1,0:T(8,128)}), (f32[512,1536]{1,0:T(8,128)}, f32[512,256]{1,0:T(8,128)}, f32[1536,512]{1,0:T(8,128)})) %all-reduce.4.cloned.1.call-update) | async-done | bytes 6815760 | tf_op jit(solution)/shard_map/psum | solution.py:913
  428.3 1.0 slice.44
  429.2 0.7 copy.86
  430.0 1.2 fusion
  431.1 0.8 copy.85
  431.9 0.8 copy.84
  432.7 2.8 convert_element_type.15
  435.5 3.0 convert_element_type.14
  438.5 1.9 copy.92
  440.4 1.0 copy.93
  441.4 1.7 copy.94
  443.0 1.4 copy-done
  444.4 1.7 copy.95
  (24 shorter events, 3.8 us)
Async XLA Ops:
  8.0 420.2 %all-reduce.4.cloned.1.call-start = ((), (), s32[]{:S(2)}) async-start(), calls=%async_computation.4 | async-start | bytes 13631488 | tf_op jit(solution)/shard_map/psum | solution.py:913
  241.3 191.4 %reduce-scatter.5.cloned.1.call-start = ((), (), s32[]{:S(2)}) async-start(), calls=%async_computation.3 | async-start | bytes 5242880 | tf_op jit(solution)/shard_map/reduce_scatter | solution.py:892
  241.9 1.3 copy-start.4
  241.9 1.3 copy-start.5
  241.9 43.0 %copy-start.3 = (f32[512,128]{1,0:T(8,128)S(1)}, f32[512,128]{1,0:T(8,128)}, u32[]{:S(2)}) copy-start(f32[512,128]{1,0:T(8,128)} %get-tuple-element.48) | copy-start | bytes 786436
  241.9 193.6 %reduce-scatter.3.cloned.1.call-start = ((), (), s32[]{:S(2)}) async-start(), calls=%async_computation.2 | async-start | bytes 5242880 | tf_op jit(solution)/shard_map/reduce_scatter | solution.py:891
  435.5 5.8 %copy-start.1 = (f32[512,1536]{1,0:T(8,128)S(1)}, f32[512,1536]{1,0:T(8,128)}, u32[]{:S(2)}) copy-start(f32[512,1536]{1,0:T(8,128)} %get-tuple-element.161) | copy-start | bytes 9437188
  435.5 4.9 %copy-start.2 = (f32[512,512]{1,0:T(8,128)S(1)}, f32[512,512]{1,0:T(8,128)}, u32[]{:S(2)}) copy-start(f32[512,512]{1,0:T(8,128)} %get-tuple-element.155) | copy-start | bytes 3145732
  441.4 3.0 copy-start
Sparse Core Ops, SparseCore 0:
  241.4 186.8 all-reduce.3
Sparse Core Ops, SparseCore 1:
  244.3 46.7 reduce-scatter.4
  293.5 43.7 reduce-scatter.2
